TPU v7x, 256 devices: a whole 4x4x8 slice. The times are simulated.
256 devices in a mesh: tgt: 32 (over z, y_hi, core), src: 8 (over y_lo, x).
Axes of the slice: x: 4, y: 4 (y_hi: 2, y_lo: 2; y = y_hi * 2 + y_lo), z: 8, core: 2. Of those that a mesh axis runs over, the one named last changes fastest.
Arguments:
- tgt_points: bfloat16 [3, 16384], P(None, 'tgt'), may hold values from -4 to 4
- tgt_weight: float32 [16384], P('tgt'), may hold values from 0.5 to 2
- src_points: bfloat16 [4, 3, 32768], P(None, None, ('tgt', 'src')), may hold values from -4 to 4
- src_weight: float32 [4, 32768], P(None, ('tgt', 'src')), may hold values from 0.5 to 2
- basis: float32 [4, 3, 32768], P(None, None, ('tgt', 'src')), may hold values from 0.05 to 1
- span: int32 [4, 32768], P(None, ('tgt', 'src')), may hold values from 0 to 29
- patch: int32 [4, 32768], P(None, ('tgt', 'src')), may hold values from 0 to 3
- patch_factor: float32 [4, 2, 1024], P(None, None, ('tgt', 'src')), may hold values from -1.5 to 1.5
- ctrl_weight: float32 [4, 8192], P(None, ('tgt', 'src')), may hold values from 0.5 to 2
- ctrl_coef: bfloat16 [4, 128, 8192], P(None, None, ('tgt', 'src')), may hold values from -6 to 6
- band: float32 [8, 16384], P(None, 'tgt'), may hold values from -0.5 to 0.5
- offsets: int32 [8], replicated, may hold values from -8 to 8, as said below
Outputs:
- shell_field: float32 [16384, 128], P('tgt')
Inputs may be any that keep to these rules, and one draw needn't show every extreme that they name: span of source point j is local to the 32 control points of the block j // 128. patch of source point j is local to the 4 patches of the block j // 128. offsets[0] is 8 and offsets[1] is -8.
All inputs are finite; a program needn't handle non-finite values.
Results may differ from a plain program's by a relative error of at most 0.0041.
Values may be sent and summed in bfloat16 or wider, within the bound.
No kernel may reach another device: no remote copies, remote signals or barrier semaphores. Data moves between devices by JAX's collectives and lax.ppermute only.
A program may use at most 128 MiB of HBM per device.

v0:
```python
import math
import jax
import jax.numpy as jnp
from jax import lax
from jax.sharding import PartitionSpec as P

HALO = 8
WAVE = 8.0
SMOOTH = 0.0025


def extended(block, sides, width):
    for axis, dim in sides:
        count = lax.axis_size(axis)
        forward = [(i, i + 1) for i in range(count - 1)]
        backward = [(target, source) for source, target in forward]
        low = lax.ppermute(
            lax.slice_in_dim(block, block.shape[dim] - width, None, axis=dim), axis, forward
        )
        high = lax.ppermute(lax.slice_in_dim(block, 0, width, axis=dim), axis, backward)
        block = jnp.concatenate([low, block, high], axis=dim)
    return block


def kernel_terms(targets, sources, density):
    tpos = targets.astype(jnp.float32)
    spos = sources.astype(jnp.float32)
    dist_sq = SMOOTH + (tpos[0][:, None] - spos[0][None, :]) ** 2
    dist_sq = dist_sq + (tpos[1][:, None] - spos[1][None, :]) ** 2
    dist_sq = dist_sq + (tpos[2][:, None] - spos[2][None, :]) ** 2
    dist = jnp.sqrt(dist_sq)
    kernel_re = (jnp.cos(WAVE * dist) / dist).astype(jnp.bfloat16)
    kernel_im = (jnp.sin(WAVE * dist) / dist).astype(jnp.bfloat16)
    dims = (((1,), (1,)), ((), ()))
    part_a = lax.dot_general(kernel_re, density, dims, preferred_element_type=jnp.float32)
    part_b = lax.dot_general(kernel_im, density, dims, preferred_element_type=jnp.float32)
    half = density.shape[0] // 2
    return jnp.concatenate(
        [part_a[:, :half] - part_b[:, half:], part_a[:, half:] + part_b[:, :half]], axis=1
    )


def block_density(weight, basis_rows, span_row, patch_row, factor_rows, weights_ctrl, coef_ctrl):
    count = weight.shape[0]
    fields = coef_ctrl.shape[0] // 2
    denom = jnp.zeros((count,), jnp.float32)
    numer = jnp.zeros((coef_ctrl.shape[0], count), jnp.float32)
    for basis_index in range(basis_rows.shape[0]):
        control_index = span_row + basis_index
        scaled = basis_rows[basis_index] * weights_ctrl[control_index]
        denom = denom + scaled
        numer = numer + scaled[None, :] * coef_ctrl[:, control_index].astype(jnp.float32)
    ratio = numer / denom[None, :]
    labels = jnp.arange(factor_rows.shape[1], dtype=jnp.int32)
    member = patch_row[None, :] == labels[:, None]
    factor_re = jnp.sum(jnp.where(member, factor_rows[0][:, None], 0.0), axis=0)
    factor_im = jnp.sum(jnp.where(member, factor_rows[1][:, None], 0.0), axis=0)
    ratio_re = ratio[:fields]
    ratio_im = ratio[fields:]
    dens_re = weight * (factor_re * ratio_re - factor_im * ratio_im)
    dens_im = weight * (factor_re * ratio_im + factor_im * ratio_re)
    return jnp.concatenate([dens_re, dens_im], axis=0).astype(jnp.bfloat16)


def add_kernel(carried, targets, geometry, density):
    width = geometry.shape[1]
    block_size = 1024

    def step_fn(index, inner):
        begin = index * block_size
        part_geo = lax.dynamic_slice_in_dim(geometry, begin, block_size, 1)
        part_den = lax.dynamic_slice_in_dim(density, begin, block_size, 1)
        return inner + kernel_terms(targets, part_geo, part_den)

    return lax.fori_loop(0, width // block_size, step_fn, carried)


def per_device(
    tgt_points,
    tgt_weight,
    src_points,
    src_weight,
    basis,
    span,
    patch,
    patch_factor,
    ctrl_weight,
    ctrl_coef,
    band,
    offsets,
):
    rows = tgt_points.shape[1]
    columns = ctrl_coef.shape[1]
    rounds = src_weight.shape[0]
    partial_value = jnp.zeros((rows, columns), jnp.float32)
    for section in range(rounds):
        density = block_density(
            src_weight[section],
            basis[section],
            span[section],
            patch[section],
            patch_factor[section],
            ctrl_weight[section],
            ctrl_coef[section],
        )
        geometry, gathered = (
            lax.all_gather(src_points[section], "tgt", axis=1, tiled=True),
            lax.all_gather(density, "tgt", axis=1, tiled=True),
        )
        partial_value = add_kernel(partial_value, tgt_points, geometry, gathered)
    total = lax.psum(partial_value, "src")
    source_count = rounds * src_weight.shape[1] * lax.axis_size("tgt") * lax.axis_size("src")
    scale = jnp.float32(1.0 / math.sqrt(source_count))
    potential = total * scale * tgt_weight[:, None]
    padded = extended(potential, (("tgt", 0),), HALO)
    shell_field = potential
    for diag in range(band.shape[0]):
        begin = HALO + offsets[diag]
        shifted = lax.dynamic_slice_in_dim(padded, begin, rows, 0)
        shell_field = shell_field + band[diag][:, None] * shifted
    return shell_field


def solution(mesh):
    in_specs = (
        P(None, "tgt"),
        P("tgt"),
        P(None, None, ("tgt", "src")),
        P(None, ("tgt", "src")),
        P(None, None, ("tgt", "src")),
        P(None, ("tgt", "src")),
        P(None, ("tgt", "src")),
        P(None, None, ("tgt", "src")),
        P(None, ("tgt", "src")),
        P(None, None, ("tgt", "src")),
        P(None, "tgt"),
        P(),
    )
    out_specs = P("tgt", None)
    return jax.shard_map(
        per_device, mesh=mesh, in_specs=in_specs, out_specs=out_specs, check_vma=False
    )
```

profile of v0, /device:TPU:1, one launch (start us, length us, event | category | flops | bytes accessed | tf_op | source)
XLA Modules:
  0.0 627.5 jit_solution(9285904822959095373)
XLA Ops:
  37.3 46.2 %all-gather = bf16[1,3,4096]{2,1,0:T(4,128)(2,1)S(1)} all-gather(bf16[1,3,128]{2,1,0:T(4,128)(2,1)S(1)} %copy.57), channel_id=2, replica_groups=mesh['tgt'=32,'src'=8] {'tgt'}, dimensions={2}, use_global_device_ids=true | all-gather | bytes 25344 | tf_op jit(solution)/shard_map/all_gather | solution.py:107
  83.5 36.7 %all-gather.1 = bf16[1,3,4096]{2,1,0:T(4,128)(2,1)S(1)} all-gather(bf16[1,3,128]{2,1,0:T(4,128)(2,1)S(1)} %copy.58), channel_id=3, replica_groups=mesh['tgt'=32,'src'=8] {'tgt'}, dimensions={2}, use_global_device_ids=true | all-gather | bytes 25344 | tf_op jit(solution)/shard_map/all_gather | solution.py:107
  120.2 39.6 %all-gather.2 = bf16[1,3,4096]{2,1,0:T(4,128)(2,1)S(1)} all-gather(bf16[1,3,128]{2,1,0:T(4,128)(2,1)S(1)} %copy.59), channel_id=4, replica_groups=mesh['tgt'=32,'src'=8] {'tgt'}, dimensions={2}, use_global_device_ids=true | all-gather | bytes 25344 | tf_op jit(solution)/shard_map/all_gather | solution.py:107
  159.8 36.7 %all-gather.3 = bf16[1,3,4096]{2,1,0:T(4,128)(2,1)S(1)} all-gather(bf16[1,3,128]{2,1,0:T(4,128)(2,1)S(1)} %copy.60), channel_id=5, replica_groups=mesh['tgt'=32,'src'=8] {'tgt'}, dimensions={2}, use_global_device_ids=true | all-gather | bytes 25344 | tf_op jit(solution)/shard_map/all_gather | solution.py:107
  196.5 78.8 %while.56 = (s32[]{:T(128)}, f32[512,128]{0,1:T(8,128)S(1)}, bf16[3,512]{1,0:T(4,128)(2,1)S(1)}, bf16[3,4096]{1,0:T(4,128)(2,1)S(1)}, bf16[128,4096]{1,0:T(8,128...) while((s32[]{:T(128)}, f32[512,128]{0,1:T(8,128)S(1)}, bf16[3,512]{1,0:T(4,128)(2,1)S(1)}, ...), condition=%wide.region_3.4_spmd.clone, body=%wide.region_2.3_spmd.clone.sunk | while | flops 281283584 | bytes 2713769 | solution.py:75
  196.7 9.7 %fusion.110 = f32[512,128]{0,1:T(8,128)S(1)} fusion(f32[1024]{0:T(1024)S(1)} %bitcast.278, f32[512]{0:T(512)S(1)} %bitcast.304, f32[1024]{0:T(1024)S(1)} %bitcast.280, f32[512]{0:T(512)S(1)} %bitcast.302, f32[1024]{0:T(1024)S(1)} %bitcast.276, f32[512]{0:T(512)S(1)} %bitcast.300, bf16[128,4096]{1,0:T(8,128)(2,1)} %get-tuple-element.859, ...), kind=kOutput, calls=%fused_computation.79.clone.1 | convolution fusion | flops 140509184 | bytes 542724 | tf_op jit(solution)/shard_map/while/body/eval_jaxpr/dot_general | solution.py:36
  216.3 9.7 %fusion.110 = f32[512,128]{0,1:T(8,128)S(1)} fusion(f32[1024]{0:T(1024)S(1)} %bitcast.278, f32[512]{0:T(512)S(1)} %bitcast.304, f32[1024]{0:T(1024)S(1)} %bitcast.280, f32[512]{0:T(512)S(1)} %bitcast.302, f32[1024]{0:T(1024)S(1)} %bitcast.276, f32[512]{0:T(512)S(1)} %bitcast.300, bf16[128,4096]{1,0:T(8,128)(2,1)} %get-tuple-element.859, ...), kind=kOutput, calls=%fused_computation.79.clone.1 | convolution fusion | flops 140509184 | bytes 542724 | tf_op jit(solution)/shard_map/while/body/eval_jaxpr/dot_general | solution.py:36
  235.8 9.7 %fusion.110 = f32[512,128]{0,1:T(8,128)S(1)} fusion(f32[1024]{0:T(1024)S(1)} %bitcast.278, f32[512]{0:T(512)S(1)} %bitcast.304, f32[1024]{0:T(1024)S(1)} %bitcast.280, f32[512]{0:T(512)S(1)} %bitcast.302, f32[1024]{0:T(1024)S(1)} %bitcast.276, f32[512]{0:T(512)S(1)} %bitcast.300, bf16[128,4096]{1,0:T(8,128)(2,1)} %get-tuple-element.859, ...), kind=kOutput, calls=%fused_computation.79.clone.1 | convolution fusion | flops 140509184 | bytes 542724 | tf_op jit(solution)/shard_map/while/body/eval_jaxpr/dot_general | solution.py:36
  255.4 9.7 %fusion.110 = f32[512,128]{0,1:T(8,128)S(1)} fusion(f32[1024]{0:T(1024)S(1)} %bitcast.278, f32[512]{0:T(512)S(1)} %bitcast.304, f32[1024]{0:T(1024)S(1)} %bitcast.280, f32[512]{0:T(512)S(1)} %bitcast.302, f32[1024]{0:T(1024)S(1)} %bitcast.276, f32[512]{0:T(512)S(1)} %bitcast.300, bf16[128,4096]{1,0:T(8,128)(2,1)} %get-tuple-element.859, ...), kind=kOutput, calls=%fused_computation.79.clone.1 | convolution fusion | flops 140509184 | bytes 542724 | tf_op jit(solution)/shard_map/while/body/eval_jaxpr/dot_general | solution.py:36
  275.3 78.1 %while.53 = (s32[]{:T(128)}, f32[512,128]{0,1:T(8,128)S(1)}, bf16[3,512]{1,0:T(4,128)(2,1)S(1)}, bf16[3,4096]{1,0:T(4,128)(2,1)S(1)}, bf16[128,4096]{1,0:T(8,128...) while((s32[]{:T(128)}, f32[512,128]{0,1:T(8,128)S(1)}, bf16[3,512]{1,0:T(4,128)(2,1)S(1)}, ...), condition=%wide.region_7.8_spmd, body=%wide.region_6.7_spmd.sunk | while | flops 281218048 | bytes 2713759 | solution.py:75
  275.4 9.7 %fusion.92 = f32[512,128]{0,1:T(8,128)S(1)} fusion(f32[1024]{0:T(1024)S(1)} %bitcast.284, f32[512]{0:T(512)S(1)} %bitcast.310, f32[1024]{0:T(1024)S(1)} %bitcast.286, f32[512]{0:T(512)S(1)} %bitcast.308, f32[1024]{0:T(1024)S(1)} %bitcast.282, f32[512]{0:T(512)S(1)} %bitcast.306, bf16[128,4096]{1,0:T(8,128)(2,1)} %get-tuple-element.886, ...), kind=kOutput, calls=%fused_computation.28.clone.1 | convolution fusion | flops 140509184 | bytes 542724 | tf_op jit(solution)/shard_map/while/body/eval_jaxpr/dot_general | solution.py:36
  294.9 9.7 %fusion.92 = f32[512,128]{0,1:T(8,128)S(1)} fusion(f32[1024]{0:T(1024)S(1)} %bitcast.284, f32[512]{0:T(512)S(1)} %bitcast.310, f32[1024]{0:T(1024)S(1)} %bitcast.286, f32[512]{0:T(512)S(1)} %bitcast.308, f32[1024]{0:T(1024)S(1)} %bitcast.282, f32[512]{0:T(512)S(1)} %bitcast.306, bf16[128,4096]{1,0:T(8,128)(2,1)} %get-tuple-element.886, ...), kind=kOutput, calls=%fused_computation.28.clone.1 | convolution fusion | flops 140509184 | bytes 542724 | tf_op jit(solution)/shard_map/while/body/eval_jaxpr/dot_general | solution.py:36
  314.5 9.7 %fusion.92 = f32[512,128]{0,1:T(8,128)S(1)} fusion(f32[1024]{0:T(1024)S(1)} %bitcast.284, f32[512]{0:T(512)S(1)} %bitcast.310, f32[1024]{0:T(1024)S(1)} %bitcast.286, f32[512]{0:T(512)S(1)} %bitcast.308, f32[1024]{0:T(1024)S(1)} %bitcast.282, f32[512]{0:T(512)S(1)} %bitcast.306, bf16[128,4096]{1,0:T(8,128)(2,1)} %get-tuple-element.886, ...), kind=kOutput, calls=%fused_computation.28.clone.1 | convolution fusion | flops 140509184 | bytes 542724 | tf_op jit(solution)/shard_map/while/body/eval_jaxpr/dot_general | solution.py:36
  334.0 9.7 %fusion.92 = f32[512,128]{0,1:T(8,128)S(1)} fusion(f32[1024]{0:T(1024)S(1)} %bitcast.284, f32[512]{0:T(512)S(1)} %bitcast.310, f32[1024]{0:T(1024)S(1)} %bitcast.286, f32[512]{0:T(512)S(1)} %bitcast.308, f32[1024]{0:T(1024)S(1)} %bitcast.282, f32[512]{0:T(512)S(1)} %bitcast.306, bf16[128,4096]{1,0:T(8,128)(2,1)} %get-tuple-element.886, ...), kind=kOutput, calls=%fused_computation.28.clone.1 | convolution fusion | flops 140509184 | bytes 542724 | tf_op jit(solution)/shard_map/while/body/eval_jaxpr/dot_general | solution.py:36
  353.5 78.3 %while.54 = (s32[]{:T(128)}, f32[512,128]{0,1:T(8,128)S(1)}, bf16[3,512]{1,0:T(4,128)(2,1)S(1)}, bf16[3,4096]{1,0:T(4,128)(2,1)S(1)}, bf16[128,4096]{1,0:T(8,128...) while((s32[]{:T(128)}, f32[512,128]{0,1:T(8,128)S(1)}, bf16[3,512]{1,0:T(4,128)(2,1)S(1)}, ...), condition=%wide.region_11.12_spmd, body=%wide.region_10.11_spmd.sunk | while | flops 281218048 | bytes 2713759 | solution.py:75
  373.3 9.7 %fusion.98 = f32[512,128]{0,1:T(8,128)S(1)} fusion(f32[1024]{0:T(1024)S(1)} %bitcast.290, f32[512]{0:T(512)S(1)} %bitcast.316, f32[1024]{0:T(1024)S(1)} %bitcast.292, f32[512]{0:T(512)S(1)} %bitcast.314, f32[1024]{0:T(1024)S(1)} %bitcast.288, f32[512]{0:T(512)S(1)} %bitcast.312, bf16[128,4096]{1,0:T(8,128)(2,1)} %get-tuple-element.913, ...), kind=kOutput, calls=%fused_computation.45.clone.1 | convolution fusion | flops 140509184 | bytes 542724 | tf_op jit(solution)/shard_map/while/body/eval_jaxpr/dot_general | solution.py:36
  392.8 9.7 %fusion.98 = f32[512,128]{0,1:T(8,128)S(1)} fusion(f32[1024]{0:T(1024)S(1)} %bitcast.290, f32[512]{0:T(512)S(1)} %bitcast.316, f32[1024]{0:T(1024)S(1)} %bitcast.292, f32[512]{0:T(512)S(1)} %bitcast.314, f32[1024]{0:T(1024)S(1)} %bitcast.288, f32[512]{0:T(512)S(1)} %bitcast.312, bf16[128,4096]{1,0:T(8,128)(2,1)} %get-tuple-element.913, ...), kind=kOutput, calls=%fused_computation.45.clone.1 | convolution fusion | flops 140509184 | bytes 542724 | tf_op jit(solution)/shard_map/while/body/eval_jaxpr/dot_general | solution.py:36
  412.3 9.7 %fusion.98 = f32[512,128]{0,1:T(8,128)S(1)} fusion(f32[1024]{0:T(1024)S(1)} %bitcast.290, f32[512]{0:T(512)S(1)} %bitcast.316, f32[1024]{0:T(1024)S(1)} %bitcast.292, f32[512]{0:T(512)S(1)} %bitcast.314, f32[1024]{0:T(1024)S(1)} %bitcast.288, f32[512]{0:T(512)S(1)} %bitcast.312, bf16[128,4096]{1,0:T(8,128)(2,1)} %get-tuple-element.913, ...), kind=kOutput, calls=%fused_computation.45.clone.1 | convolution fusion | flops 140509184 | bytes 542724 | tf_op jit(solution)/shard_map/while/body/eval_jaxpr/dot_general | solution.py:36
  431.8 91.2 %while.55 = (s32[]{:T(128)}, f32[512,128]{0,1:T(8,128)S(1)}, bf16[3,512]{1,0:T(4,128)(2,1)S(1)}, bf16[3,4096]{1,0:T(4,128)(2,1)S(1)}, bf16[128,4096]{1,0:T(8,128...) while((s32[]{:T(128)}, f32[512,128]{0,1:T(8,128)S(1)}, bf16[3,512]{1,0:T(4,128)(2,1)S(1)}, ...), condition=%wide.region_15.16_spmd, body=%wide.region_14.15_spmd.sunk | while | flops 281218048 | bytes 2713759 | solution.py:75
  445.0 9.7 %fusion.104 = f32[512,128]{0,1:T(8,128)S(1)} fusion(f32[1024]{0:T(1024)S(1)} %bitcast.296, f32[512]{0:T(512)S(1)} %bitcast.322, f32[1024]{0:T(1024)S(1)} %bitcast.298, f32[512]{0:T(512)S(1)} %bitcast.320, f32[1024]{0:T(1024)S(1)} %bitcast.294, f32[512]{0:T(512)S(1)} %bitcast.318, bf16[128,4096]{1,0:T(8,128)(2,1)} %get-tuple-element.940, ...), kind=kOutput, calls=%fused_computation.62.clone.1 | convolution fusion | flops 140509184 | bytes 542724 | tf_op jit(solution)/shard_map/while/body/eval_jaxpr/dot_general | solution.py:36
  464.5 9.7 %fusion.104 = f32[512,128]{0,1:T(8,128)S(1)} fusion(f32[1024]{0:T(1024)S(1)} %bitcast.296, f32[512]{0:T(512)S(1)} %bitcast.322, f32[1024]{0:T(1024)S(1)} %bitcast.298, f32[512]{0:T(512)S(1)} %bitcast.320, f32[1024]{0:T(1024)S(1)} %bitcast.294, f32[512]{0:T(512)S(1)} %bitcast.318, bf16[128,4096]{1,0:T(8,128)(2,1)} %get-tuple-element.940, ...), kind=kOutput, calls=%fused_computation.62.clone.1 | convolution fusion | flops 140509184 | bytes 542724 | tf_op jit(solution)/shard_map/while/body/eval_jaxpr/dot_general | solution.py:36
  484.1 9.7 %fusion.104 = f32[512,128]{0,1:T(8,128)S(1)} fusion(f32[1024]{0:T(1024)S(1)} %bitcast.296, f32[512]{0:T(512)S(1)} %bitcast.322, f32[1024]{0:T(1024)S(1)} %bitcast.298, f32[512]{0:T(512)S(1)} %bitcast.320, f32[1024]{0:T(1024)S(1)} %bitcast.294, f32[512]{0:T(512)S(1)} %bitcast.318, bf16[128,4096]{1,0:T(8,128)(2,1)} %get-tuple-element.940, ...), kind=kOutput, calls=%fused_computation.62.clone.1 | convolution fusion | flops 140509184 | bytes 542724 | tf_op jit(solution)/shard_map/while/body/eval_jaxpr/dot_general | solution.py:36
  503.6 9.7 %fusion.104 = f32[512,128]{0,1:T(8,128)S(1)} fusion(f32[1024]{0:T(1024)S(1)} %bitcast.296, f32[512]{0:T(512)S(1)} %bitcast.322, f32[1024]{0:T(1024)S(1)} %bitcast.298, f32[512]{0:T(512)S(1)} %bitcast.320, f32[1024]{0:T(1024)S(1)} %bitcast.294, f32[512]{0:T(512)S(1)} %bitcast.318, bf16[128,4096]{1,0:T(8,128)(2,1)} %get-tuple-element.940, ...), kind=kOutput, calls=%fused_computation.62.clone.1 | convolution fusion | flops 140509184 | bytes 542724 | tf_op jit(solution)/shard_map/while/body/eval_jaxpr/dot_general | solution.py:36
  524.0 71.3 %all-reduce.2.cloned.1.call-done = f32[512,128]{1,0:T(8,128)} async-done(((f32[512,128]{1,0:T(8,128)}), f32[512,128]{1,0:T(8,128)}) %all-reduce.2.cloned.1.call-update) | async-done | bytes 262160 | tf_op jit(solution)/shard_map/psum | solution.py:111
  (213 shorter events, 212.5 us)
Async XLA Ops:
  6.5 190.0 %all-gather.9.cloned.1.call-start = ((), (), s32[]{:S(2)}) async-start(), calls=%async_computation | async-start | bytes 1081344 | tf_op jit(solution)/shard_map/all_gather | solution.py:108
  17.7 5.0 copy-start.6
  17.7 5.0 copy-start.7
  17.7 5.0 copy-start.8
  17.7 5.1 copy-start.5
  23.6 251.7 %all-gather.11.cloned.1.call-start = ((), (), s32[]{:S(2)}) async-start(), calls=%async_computation.1 | async-start | bytes 1081344 | tf_op jit(solution)/shard_map/all_gather | solution.py:108
  26.8 326.6 %all-gather.13.cloned.1.call-start = ((), (), s32[]{:S(2)}) async-start(), calls=%async_computation.2 | async-start | bytes 1081344 | tf_op jit(solution)/shard_map/all_gather | solution.py:108
  32.7 4.5 copy-start.4
  33.0 163.5 %copy-start = (bf16[3,512]{1,0:T(4,128)(2,1)S(1)}, bf16[3,512]{1,0:T(4,128)(2,1)}, u32[]{:S(2)}) copy-start(bf16[3,512]{1,0:T(4,128)(2,1)} %param.20) | copy-start | bytes 9220
  33.9 397.9 %all-gather.15.cloned.1.call-start = ((), (), s32[]{:S(2)}) async-start(), calls=%async_computation.3 | async-start | bytes 1081344 | tf_op jit(solution)/shard_map/all_gather | solution.py:108
  37.2 558.2 %all-reduce.2.cloned.1.call-start = ((), (), s32[]{:S(2)}) async-start(), calls=%async_computation.4 | async-start | bytes 524288 | tf_op jit(solution)/shard_map/psum | solution.py:111
  431.8 92.1 %copy-start.9 = (f32[512]{0:T(512)S(1)}, f32[512]{0:T(512)}, u32[]{:S(2)}) copy-start(f32[512]{0:T(512)} %param.21) | copy-start | bytes 6148
  431.8 92.1 %copy-start.3 = (f32[8,512]{1,0:T(8,128)S(1)}, f32[8,512]{1,0:T(8,128)}, u32[]{:S(2)}) copy-start(f32[8,512]{1,0:T(8,128)} %param.30) | copy-start | bytes 49156
  523.1 85.2 %copy-start.2 = (s32[8]{0:T(128)S(1)}, s32[8]{0:T(128)}, u32[]{:S(2)}) copy-start(s32[8]{0:T(128)} %param.31) | copy-start | bytes 100
  595.3 23.9 %copy-start.1 = (f32[512,128]{1,0:T(8,128)S(1)}, f32[512,128]{1,0:T(8,128)}, u32[]{:S(2)}) copy-start(f32[512,128]{1,0:T(8,128)} %all-reduce.2.cloned.1.call-done) | copy-start | bytes 786436
  596.5 22.7 %collective-permute-start.1 = (f32[8,128]{1,0:T(8,128)S(1)}, f32[8,128]{1,0:T(8,128)S(1)}, u32[]{:S(2)}, u32[]{:S(2)}) collective-permute-start(f32[8,128]{1,0:T(8,128)S(1)} %get-tuple-element.560), channel_id=1, source_target_pairs={{8,0},{16,8},{24,16},{32,24},{40,32},{48,40},{56,48},{64,56},{72,6... | collective-permute-start | bytes 12296 | tf_op jit(solution)/shard_map/ppermute | solution.py:20
  604.0 15.2 %collective-permute-start = (f32[8,128]{1,0:T(8,128)S(1)}, f32[8,128]{1,0:T(8,128)S(1)}, u32[]{:S(2)}, u32[]{:S(2)}) collective-permute-start(f32[8,128]{1,0:T(8,128)S(1)} %get-tuple-element.559), channel_id=1, source_target_pairs={{0,8},{8,16},{16,24},{24,32},{32,40},{40,48},{48,56},{56,64},{64,7... | collective-permute-start | bytes 12296 | tf_op jit(solution)/shard_map/ppermute | solution.py:17
Sparse Core Ops, SparseCore 0:
  23.7 76.4 all-gather.8
  102.7 70.0 all-gather.10
  175.4 69.8 all-gather.12
  247.7 69.9 all-gather.14
  524.1 71.2 all-reduce.1
where the time goes:
time: 635 us; the launch traced here: 628 us
  matrix products  309 us (49%)
  blocking collectives  159 us (25%)
  waiting for transfers between devices  71.5 us (11%)
  local copies, waits for them, and re-layouts  28.2 us (4%)
  between operations  24.2 us (4%)
  loops' own time  15.1 us (2%)
  starting transfers between devices  11.9 us (2%)
  other arithmetic  8.44 us (1%)
    all_gather x4, blocking collectives, per_device(): lax.all_gather(src_points[section], 'tgt', axis=1, tiled=True)  159 us
    dot_general x16, matrix products, kernel_terms(): lax.dot_general(kernel_im, density, dims, preferred_element_type=jnp.floa...  155 us
    dot_general x16, matrix products, kernel_terms(): lax.dot_general(kernel_re, density, dims, preferred_element_type=jnp.floa...  154 us
    psum x1, waiting for transfers between devices, per_device(): total = lax.psum(partial_value, 'src')  71.3 us
    another operation x4, loops' own time, add_kernel(): return lax.fori_loop(0, width // block_size, step_fn, carried)  15.1 us
    gather x12, local copies, waits for them, and re-layouts, block_density(): scaled = basis_rows[basis_index] * weights_ctrl[control_index]  14.7 us
  transfers between devices with their start and end apart: 7, of which 1 were waited for; matrix products, arithmetic and copies ran while one was open for 39% of the time, Pallas kernels for 0%

commit v1 on v0

--- a/solution.py
+++ b/solution.py
@@ -108,7 +108,7 @@
             lax.all_gather(density, "tgt", axis=1, tiled=True),
         )
         partial_value = add_kernel(partial_value, tgt_points, geometry, gathered)
-    total = lax.psum(partial_value, "src")
+    total = jnp.sum(lax.all_gather(partial_value, "src"), axis=0)
     source_count = rounds * src_weight.shape[1] * lax.axis_size("tgt") * lax.axis_size("src")
     scale = jnp.float32(1.0 / math.sqrt(source_count))
     potential = total * scale * tgt_weight[:, None]

time: 635 us -> 590 us (0.929)
  waiting for transfers between devices: 71.5 us -> 36.7 us
  loops' own time: 15.1 us -> 2.51 us
    psum x1 -> x0, waiting for transfers between devices: 71.3 us -> none  [per_device(): total = lax.psum(partial_value, 'src')]
    all_gather x0 -> x1, waiting for transfers between devices: none -> 36.5 us  [per_device(): total = jnp.sum(lax.all_gather(partial_value, 'src'), axis=0)]
    another operation x4, loops' own time: 15.1 us -> 2.51 us  [add_kernel(): return lax.fori_loop(0, width // block_size, step_fn, carried)]
  transfers between devices with their start and end apart: 7 -> 7, of which waited for: 1 -> 1; matrix products, arithmetic and copies ran while one was open for 39% -> 42% of each run, Pallas kernels for 0% -> 0%
where the time goes in v1:
time: 590 us; the launch traced here: 583 us
  matrix products  309 us (52%)
  blocking collectives  159 us (27%)
  waiting for transfers between devices  36.7 us (6%)
  local copies, waits for them, and re-layouts  32.1 us (5%)
  between operations  23.8 us (4%)
  starting transfers between devices  12 us (2%)
  other arithmetic  7.1 us (1%)
    all_gather x4, blocking collectives, per_device(): lax.all_gather(src_points[section], 'tgt', axis=1, tiled=True)  159 us
    dot_general x16, matrix products, kernel_terms(): lax.dot_general(kernel_im, density, dims, preferred_element_type=jnp.floa...  155 us
    dot_general x16, matrix products, kernel_terms(): lax.dot_general(kernel_re, density, dims, preferred_element_type=jnp.floa...  154 us
    all_gather x1, waiting for transfers between devices, per_device(): total = jnp.sum(lax.all_gather(partial_value, 'src'), axis=0)  36.5 us
    gather x12, local copies, waits for them, and re-layouts, block_density(): scaled = basis_rows[basis_index] * weights_ctrl[control_index]  14.7 us
  transfers between devices with their start and end apart: 7, of which 1 were waited for; matrix products, arithmetic and copies ran while one was open for 42% of the time, Pallas kernels for 0%

profile of v1, /device:TPU:1, one launch (start us, length us, event | category | flops | bytes accessed | tf_op | source)
XLA Modules:
  0.0 582.6 jit_solution(13544731527268991876)
XLA Ops:
  37.3 46.2 %all-gather = bf16[1,3,4096]{2,1,0:T(4,128)(2,1)S(1)} all-gather(bf16[1,3,128]{2,1,0:T(4,128)(2,1)S(1)} %copy.64), channel_id=2, replica_groups=mesh['tgt'=32,'src'=8] {'tgt'}, dimensions={2}, use_global_device_ids=true | all-gather | bytes 25344 | tf_op jit(solution)/shard_map/all_gather | solution.py:107
  83.5 36.7 %all-gather.1 = bf16[1,3,4096]{2,1,0:T(4,128)(2,1)S(1)} all-gather(bf16[1,3,128]{2,1,0:T(4,128)(2,1)S(1)} %copy.65), channel_id=3, replica_groups=mesh['tgt'=32,'src'=8] {'tgt'}, dimensions={2}, use_global_device_ids=true | all-gather | bytes 25344 | tf_op jit(solution)/shard_map/all_gather | solution.py:107
  120.2 39.6 %all-gather.2 = bf16[1,3,4096]{2,1,0:T(4,128)(2,1)S(1)} all-gather(bf16[1,3,128]{2,1,0:T(4,128)(2,1)S(1)} %copy.66), channel_id=4, replica_groups=mesh['tgt'=32,'src'=8] {'tgt'}, dimensions={2}, use_global_device_ids=true | all-gather | bytes 25344 | tf_op jit(solution)/shard_map/all_gather | solution.py:107
  159.8 36.7 %all-gather.3 = bf16[1,3,4096]{2,1,0:T(4,128)(2,1)S(1)} all-gather(bf16[1,3,128]{2,1,0:T(4,128)(2,1)S(1)} %copy.67), channel_id=5, replica_groups=mesh['tgt'=32,'src'=8] {'tgt'}, dimensions={2}, use_global_device_ids=true | all-gather | bytes 25344 | tf_op jit(solution)/shard_map/all_gather | solution.py:107
  196.5 78.8 %while.56 = (s32[]{:T(128)}, f32[512,128]{0,1:T(8,128)S(1)}, bf16[3,512]{1,0:T(4,128)(2,1)S(1)}, bf16[3,4096]{1,0:T(4,128)(2,1)S(1)}, bf16[128,4096]{1,0:T(8,128...) while((s32[]{:T(128)}, f32[512,128]{0,1:T(8,128)S(1)}, bf16[3,512]{1,0:T(4,128)(2,1)S(1)}, ...), condition=%wide.region_3.4_spmd.clone, body=%wide.region_2.3_spmd.clone.sunk | while | flops 281283584 | bytes 2713769 | solution.py:75
  196.7 9.7 %fusion.110 = f32[512,128]{0,1:T(8,128)S(1)} fusion(f32[1024]{0:T(1024)S(1)} %bitcast.284, f32[512]{0:T(512)S(1)} %bitcast.310, f32[1024]{0:T(1024)S(1)} %bitcast.286, f32[512]{0:T(512)S(1)} %bitcast.308, f32[1024]{0:T(1024)S(1)} %bitcast.282, f32[512]{0:T(512)S(1)} %bitcast.306, bf16[128,4096]{1,0:T(8,128)(2,1)} %get-tuple-element.879, ...), kind=kOutput, calls=%fused_computation.79.clone.1 | convolution fusion | flops 140509184 | bytes 542724 | tf_op jit(solution)/shard_map/while/body/eval_jaxpr/dot_general | solution.py:36
  216.3 9.7 %fusion.110 = f32[512,128]{0,1:T(8,128)S(1)} fusion(f32[1024]{0:T(1024)S(1)} %bitcast.284, f32[512]{0:T(512)S(1)} %bitcast.310, f32[1024]{0:T(1024)S(1)} %bitcast.286, f32[512]{0:T(512)S(1)} %bitcast.308, f32[1024]{0:T(1024)S(1)} %bitcast.282, f32[512]{0:T(512)S(1)} %bitcast.306, bf16[128,4096]{1,0:T(8,128)(2,1)} %get-tuple-element.879, ...), kind=kOutput, calls=%fused_computation.79.clone.1 | convolution fusion | flops 140509184 | bytes 542724 | tf_op jit(solution)/shard_map/while/body/eval_jaxpr/dot_general | solution.py:36
  235.8 9.7 %fusion.110 = f32[512,128]{0,1:T(8,128)S(1)} fusion(f32[1024]{0:T(1024)S(1)} %bitcast.284, f32[512]{0:T(512)S(1)} %bitcast.310, f32[1024]{0:T(1024)S(1)} %bitcast.286, f32[512]{0:T(512)S(1)} %bitcast.308, f32[1024]{0:T(1024)S(1)} %bitcast.282, f32[512]{0:T(512)S(1)} %bitcast.306, bf16[128,4096]{1,0:T(8,128)(2,1)} %get-tuple-element.879, ...), kind=kOutput, calls=%fused_computation.79.clone.1 | convolution fusion | flops 140509184 | bytes 542724 | tf_op jit(solution)/shard_map/while/body/eval_jaxpr/dot_general | solution.py:36
  255.4 9.7 %fusion.110 = f32[512,128]{0,1:T(8,128)S(1)} fusion(f32[1024]{0:T(1024)S(1)} %bitcast.284, f32[512]{0:T(512)S(1)} %bitcast.310, f32[1024]{0:T(1024)S(1)} %bitcast.286, f32[512]{0:T(512)S(1)} %bitcast.308, f32[1024]{0:T(1024)S(1)} %bitcast.282, f32[512]{0:T(512)S(1)} %bitcast.306, bf16[128,4096]{1,0:T(8,128)(2,1)} %get-tuple-element.879, ...), kind=kOutput, calls=%fused_computation.79.clone.1 | convolution fusion | flops 140509184 | bytes 542724 | tf_op jit(solution)/shard_map/while/body/eval_jaxpr/dot_general | solution.py:36
  275.3 78.1 %while.53 = (s32[]{:T(128)}, f32[512,128]{0,1:T(8,128)S(1)}, bf16[3,512]{1,0:T(4,128)(2,1)S(1)}, bf16[3,4096]{1,0:T(4,128)(2,1)S(1)}, bf16[128,4096]{1,0:T(8,128...) while((s32[]{:T(128)}, f32[512,128]{0,1:T(8,128)S(1)}, bf16[3,512]{1,0:T(4,128)(2,1)S(1)}, ...), condition=%wide.region_7.8_spmd, body=%wide.region_6.7_spmd.sunk | while | flops 281218048 | bytes 2713759 | solution.py:75
  275.4 9.7 %fusion.92 = f32[512,128]{0,1:T(8,128)S(1)} fusion(f32[1024]{0:T(1024)S(1)} %bitcast.290, f32[512]{0:T(512)S(1)} %bitcast.316, f32[1024]{0:T(1024)S(1)} %bitcast.292, f32[512]{0:T(512)S(1)} %bitcast.314, f32[1024]{0:T(1024)S(1)} %bitcast.288, f32[512]{0:T(512)S(1)} %bitcast.312, bf16[128,4096]{1,0:T(8,128)(2,1)} %get-tuple-element.906, ...), kind=kOutput, calls=%fused_computation.28.clone.1 | convolution fusion | flops 140509184 | bytes 542724 | tf_op jit(solution)/shard_map/while/body/eval_jaxpr/dot_general | solution.py:36
  294.9 9.7 %fusion.92 = f32[512,128]{0,1:T(8,128)S(1)} fusion(f32[1024]{0:T(1024)S(1)} %bitcast.290, f32[512]{0:T(512)S(1)} %bitcast.316, f32[1024]{0:T(1024)S(1)} %bitcast.292, f32[512]{0:T(512)S(1)} %bitcast.314, f32[1024]{0:T(1024)S(1)} %bitcast.288, f32[512]{0:T(512)S(1)} %bitcast.312, bf16[128,4096]{1,0:T(8,128)(2,1)} %get-tuple-element.906, ...), kind=kOutput, calls=%fused_computation.28.clone.1 | convolution fusion | flops 140509184 | bytes 542724 | tf_op jit(solution)/shard_map/while/body/eval_jaxpr/dot_general | solution.py:36
  314.4 9.7 %fusion.92 = f32[512,128]{0,1:T(8,128)S(1)} fusion(f32[1024]{0:T(1024)S(1)} %bitcast.290, f32[512]{0:T(512)S(1)} %bitcast.316, f32[1024]{0:T(1024)S(1)} %bitcast.292, f32[512]{0:T(512)S(1)} %bitcast.314, f32[1024]{0:T(1024)S(1)} %bitcast.288, f32[512]{0:T(512)S(1)} %bitcast.312, bf16[128,4096]{1,0:T(8,128)(2,1)} %get-tuple-element.906, ...), kind=kOutput, calls=%fused_computation.28.clone.1 | convolution fusion | flops 140509184 | bytes 542724 | tf_op jit(solution)/shard_map/while/body/eval_jaxpr/dot_general | solution.py:36
  334.0 9.7 %fusion.92 = f32[512,128]{0,1:T(8,128)S(1)} fusion(f32[1024]{0:T(1024)S(1)} %bitcast.290, f32[512]{0:T(512)S(1)} %bitcast.316, f32[1024]{0:T(1024)S(1)} %bitcast.292, f32[512]{0:T(512)S(1)} %bitcast.314, f32[1024]{0:T(1024)S(1)} %bitcast.288, f32[512]{0:T(512)S(1)} %bitcast.312, bf16[128,4096]{1,0:T(8,128)(2,1)} %get-tuple-element.906, ...), kind=kOutput, calls=%fused_computation.28.clone.1 | convolution fusion | flops 140509184 | bytes 542724 | tf_op jit(solution)/shard_map/while/body/eval_jaxpr/dot_general | solution.py:36
  353.5 78.3 %while.54 = (s32[]{:T(128)}, f32[512,128]{0,1:T(8,128)S(1)}, bf16[3,512]{1,0:T(4,128)(2,1)S(1)}, bf16[3,4096]{1,0:T(4,128)(2,1)S(1)}, bf16[128,4096]{1,0:T(8,128...) while((s32[]{:T(128)}, f32[512,128]{0,1:T(8,128)S(1)}, bf16[3,512]{1,0:T(4,128)(2,1)S(1)}, ...), condition=%wide.region_11.12_spmd, body=%wide.region_10.11_spmd.sunk | while | flops 281218048 | bytes 2713759 | solution.py:75
  373.2 9.7 %fusion.98 = f32[512,128]{0,1:T(8,128)S(1)} fusion(f32[1024]{0:T(1024)S(1)} %bitcast.296, f32[512]{0:T(512)S(1)} %bitcast.322, f32[1024]{0:T(1024)S(1)} %bitcast.298, f32[512]{0:T(512)S(1)} %bitcast.320, f32[1024]{0:T(1024)S(1)} %bitcast.294, f32[512]{0:T(512)S(1)} %bitcast.318, bf16[128,4096]{1,0:T(8,128)(2,1)} %get-tuple-element.933, ...), kind=kOutput, calls=%fused_computation.45.clone.1 | convolution fusion | flops 140509184 | bytes 542724 | tf_op jit(solution)/shard_map/while/body/eval_jaxpr/dot_general | solution.py:36
  392.8 9.7 %fusion.98 = f32[512,128]{0,1:T(8,128)S(1)} fusion(f32[1024]{0:T(1024)S(1)} %bitcast.296, f32[512]{0:T(512)S(1)} %bitcast.322, f32[1024]{0:T(1024)S(1)} %bitcast.298, f32[512]{0:T(512)S(1)} %bitcast.320, f32[1024]{0:T(1024)S(1)} %bitcast.294, f32[512]{0:T(512)S(1)} %bitcast.318, bf16[128,4096]{1,0:T(8,128)(2,1)} %get-tuple-element.933, ...), kind=kOutput, calls=%fused_computation.45.clone.1 | convolution fusion | flops 140509184 | bytes 542724 | tf_op jit(solution)/shard_map/while/body/eval_jaxpr/dot_general | solution.py:36
  412.3 9.7 %fusion.98 = f32[512,128]{0,1:T(8,128)S(1)} fusion(f32[1024]{0:T(1024)S(1)} %bitcast.296, f32[512]{0:T(512)S(1)} %bitcast.322, f32[1024]{0:T(1024)S(1)} %bitcast.298, f32[512]{0:T(512)S(1)} %bitcast.320, f32[1024]{0:T(1024)S(1)} %bitcast.294, f32[512]{0:T(512)S(1)} %bitcast.318, bf16[128,4096]{1,0:T(8,128)(2,1)} %get-tuple-element.933, ...), kind=kOutput, calls=%fused_computation.45.clone.1 | convolution fusion | flops 140509184 | bytes 542724 | tf_op jit(solution)/shard_map/while/body/eval_jaxpr/dot_general | solution.py:36
  431.8 78.7 %while.55 = (s32[]{:T(128)}, f32[512,128]{0,1:T(8,128)S(1)}, bf16[3,512]{1,0:T(4,128)(2,1)S(1)}, bf16[3,4096]{1,0:T(4,128)(2,1)S(1)}, bf16[128,4096]{1,0:T(8,128...) while((s32[]{:T(128)}, f32[512,128]{0,1:T(8,128)S(1)}, bf16[3,512]{1,0:T(4,128)(2,1)S(1)}, ...), condition=%wide.region_15.16_spmd, body=%wide.region_14.15_spmd.sunk | while | flops 281218048 | bytes 2713759 | solution.py:75
  432.3 9.7 %fusion.104 = f32[512,128]{0,1:T(8,128)S(1)} fusion(f32[1024]{0:T(1024)S(1)} %bitcast.302, f32[512]{0:T(512)S(1)} %bitcast.328, f32[1024]{0:T(1024)S(1)} %bitcast.304, f32[512]{0:T(512)S(1)} %bitcast.326, f32[1024]{0:T(1024)S(1)} %bitcast.300, f32[512]{0:T(512)S(1)} %bitcast.324, bf16[128,4096]{1,0:T(8,128)(2,1)} %get-tuple-element.960, ...), kind=kOutput, calls=%fused_computation.62.clone.1 | convolution fusion | flops 140509184 | bytes 542724 | tf_op jit(solution)/shard_map/while/body/eval_jaxpr/dot_general | solution.py:36
  451.8 9.7 %fusion.104 = f32[512,128]{0,1:T(8,128)S(1)} fusion(f32[1024]{0:T(1024)S(1)} %bitcast.302, f32[512]{0:T(512)S(1)} %bitcast.328, f32[1024]{0:T(1024)S(1)} %bitcast.304, f32[512]{0:T(512)S(1)} %bitcast.326, f32[1024]{0:T(1024)S(1)} %bitcast.300, f32[512]{0:T(512)S(1)} %bitcast.324, bf16[128,4096]{1,0:T(8,128)(2,1)} %get-tuple-element.960, ...), kind=kOutput, calls=%fused_computation.62.clone.1 | convolution fusion | flops 140509184 | bytes 542724 | tf_op jit(solution)/shard_map/while/body/eval_jaxpr/dot_general | solution.py:36
  471.3 9.7 %fusion.104 = f32[512,128]{0,1:T(8,128)S(1)} fusion(f32[1024]{0:T(1024)S(1)} %bitcast.302, f32[512]{0:T(512)S(1)} %bitcast.328, f32[1024]{0:T(1024)S(1)} %bitcast.304, f32[512]{0:T(512)S(1)} %bitcast.326, f32[1024]{0:T(1024)S(1)} %bitcast.300, f32[512]{0:T(512)S(1)} %bitcast.324, bf16[128,4096]{1,0:T(8,128)(2,1)} %get-tuple-element.960, ...), kind=kOutput, calls=%fused_computation.62.clone.1 | convolution fusion | flops 140509184 | bytes 542724 | tf_op jit(solution)/shard_map/while/body/eval_jaxpr/dot_general | solution.py:36
  490.9 9.7 %fusion.104 = f32[512,128]{0,1:T(8,128)S(1)} fusion(f32[1024]{0:T(1024)S(1)} %bitcast.302, f32[512]{0:T(512)S(1)} %bitcast.328, f32[1024]{0:T(1024)S(1)} %bitcast.304, f32[512]{0:T(512)S(1)} %bitcast.326, f32[1024]{0:T(1024)S(1)} %bitcast.300, f32[512]{0:T(512)S(1)} %bitcast.324, bf16[128,4096]{1,0:T(8,128)(2,1)} %get-tuple-element.960, ...), kind=kOutput, calls=%fused_computation.62.clone.1 | convolution fusion | flops 140509184 | bytes 542724 | tf_op jit(solution)/shard_map/while/body/eval_jaxpr/dot_general | solution.py:36
  511.3 36.5 %all-gather.19.cloned.1.call-done = f32[4096,128]{0,1:T(8,128)} async-done(((f32[512,128]{0,1:T(8,128)}), f32[4096,128]{0,1:T(8,128)}) %all-gather.19.cloned.1.call-update) | async-done | bytes 2097168 | tf_op jit(solution)/shard_map/all_gather | solution.py:111
  (215 shorter events, 215.2 us)
Async XLA Ops:
  6.5 190.0 %all-gather.11.cloned.1.call-start = ((), (), s32[]{:S(2)}) async-start(), calls=%async_computation | async-start | bytes 1081344 | tf_op jit(solution)/shard_map/all_gather | solution.py:108
  12.9 9.8 %copy-start.6 = (f32[4,2,4]{2,1,0:T(2,128)S(1)}, f32[4,2,4]{2,1,0:T(2,128)}, u32[]{:S(2)}) copy-start(f32[4,2,4]{2,1,0:T(2,128)} %param.27) | copy-start | bytes 388
  12.9 9.8 %copy-start.7 = (s32[4,128]{1,0:T(4,128)S(1)}, s32[4,128]{1,0:T(4,128)}, u32[]{:S(2)}) copy-start(s32[4,128]{1,0:T(4,128)} %param.26) | copy-start | bytes 6148
  12.9 9.8 %copy-start.8 = (f32[4,128]{1,0:T(4,128)S(1)}, f32[4,128]{1,0:T(4,128)}, u32[]{:S(2)}) copy-start(f32[4,128]{1,0:T(4,128)} %param.23) | copy-start | bytes 6148
  12.9 9.9 %copy-start.5 = (f32[4,3,128]{2,0,1:T(4,128)S(1)}, f32[4,3,128]{2,0,1:T(4,128)}, u32[]{:S(2)}) copy-start(f32[4,3,128]{2,0,1:T(4,128)} %param.24) | copy-start | bytes 18436
  23.6 251.7 %all-gather.13.cloned.1.call-start = ((), (), s32[]{:S(2)}) async-start(), calls=%async_computation.1 | async-start | bytes 1081344 | tf_op jit(solution)/shard_map/all_gather | solution.py:108
  26.8 326.6 %all-gather.15.cloned.1.call-start = ((), (), s32[]{:S(2)}) async-start(), calls=%async_computation.2 | async-start | bytes 1081344 | tf_op jit(solution)/shard_map/all_gather | solution.py:108
  27.6 9.6 %copy-start.4 = (bf16[4,3,128]{2,0,1:T(4,128)(2,1)S(1)}, bf16[4,3,128]{2,0,1:T(4,128)(2,1)}, u32[]{:S(2)}) copy-start(bf16[4,3,128]{2,0,1:T(4,128)(2,1)} %param.22) | copy-start | bytes 9220
  28.3 168.2 %copy-start.1 = (bf16[3,512]{1,0:T(4,128)(2,1)S(1)}, bf16[3,512]{1,0:T(4,128)(2,1)}, u32[]{:S(2)}) copy-start(bf16[3,512]{1,0:T(4,128)(2,1)} %param.20) | copy-start | bytes 9220
  33.9 397.9 %all-gather.17.cloned.1.call-start = ((), (), s32[]{:S(2)}) async-start(), calls=%async_computation.3 | async-start | bytes 1081344 | tf_op jit(solution)/shard_map/all_gather | solution.py:108
  37.2 510.7 %all-gather.19.cloned.1.call-start = ((), (), s32[]{:S(2)}) async-start(), calls=%async_computation.4 | async-start | bytes 2359296 | tf_op jit(solution)/shard_map/all_gather | solution.py:111
  431.8 79.5 %copy-start.9 = (f32[512]{0:T(512)S(1)}, f32[512]{0:T(512)}, u32[]{:S(2)}) copy-start(f32[512]{0:T(512)} %param.21) | copy-start | bytes 6148
  431.8 79.5 %copy-start.3 = (f32[8,512]{1,0:T(8,128)S(1)}, f32[8,512]{1,0:T(8,128)}, u32[]{:S(2)}) copy-start(f32[8,512]{1,0:T(8,128)} %param.30) | copy-start | bytes 49156
  510.5 0.7 copy-start
  551.1 12.5 %copy-start.2 = (s32[8]{0:T(128)S(1)}, s32[8]{0:T(128)}, u32[]{:S(2)}) copy-start(s32[8]{0:T(128)} %param.31) | copy-start | bytes 100
  551.7 22.5 %collective-permute-start.1 = (f32[8,128]{0,1:T(8,128)S(1)}, f32[8,128]{0,1:T(8,128)S(1)}, u32[]{:S(2)}, u32[]{:S(2)}) collective-permute-start(f32[8,128]{0,1:T(8,128)S(1)} %get-tuple-element.580), channel_id=1, source_target_pairs={{8,0},{16,8},{24,16},{32,24},{40,32},{48,40},{56,48},{64,56},{72,6... | collective-permute-start | bytes 12296 | tf_op jit(solution)/shard_map/ppermute | solution.py:20
  559.3 14.9 %collective-permute-start = (f32[8,128]{0,1:T(8,128)S(1)}, f32[8,128]{0,1:T(8,128)S(1)}, u32[]{:S(2)}, u32[]{:S(2)}) collective-permute-start(f32[8,128]{0,1:T(8,128)S(1)} %get-tuple-element.579), channel_id=1, source_target_pairs={{0,8},{8,16},{16,24},{24,32},{32,40},{40,48},{48,56},{56,64},{64,7... | collective-permute-start | bytes 12296 | tf_op jit(solution)/shard_map/ppermute | solution.py:17
Sparse Core Ops, SparseCore 0:
  23.7 76.4 all-gather.10
  102.7 70.0 all-gather.12
  175.4 69.8 all-gather.14
  247.7 69.9 all-gather.16
  511.4 36.4 all-gather.18
